TPU v7x, 256 devices: a whole 4x4x8 slice. The times are simulated.
256 devices in a mesh: tm: 16 (over x, z_hi, core), input: 16 (over z_lo, y).
Axes of the slice: x: 4, y: 4, z: 8 (z_hi: 2, z_lo: 4; z = z_hi * 4 + z_lo), core: 2. Of those that a mesh axis runs over, the one named last changes fastest.
Arguments:
- samples: bfloat16 [2, 262144, 2048], P(None, 'tm', 'input'), may hold values from -6 to 6
- filter_taps: float32 [16, 1024], replicated, may hold values from -1.5 to 1.5
Outputs:
- visibilities: bfloat16 [2, 64, 2048, 2048], P(None, 'tm', 'input')
All inputs are finite; a program needn't handle non-finite values.
Results may differ from a plain program's by a relative error of at most 0.0056.
Values may be sent and summed in bfloat16 or wider, within the bound.
A program may use at most 192 MiB of HBM per device.

v0:
```python
import jax
import jax.numpy as jnp
from jax import lax
from jax.sharding import PartitionSpec as P

CH_DEV = 4


def passed_along(shard, axis, by):
    size = lax.axis_size(axis)
    pairs = [(i, i + by) for i in range(size) if 0 <= i + by < size]
    return lax.ppermute(shard, axis, pairs)


def dft_table(count, length):
    chan = jnp.arange(count, dtype=jnp.int32)
    point = jnp.arange(length, dtype=jnp.int32)
    phase = chan[:, None] * point[None, :] % length
    theta = 2.0 * jnp.pi / length * phase.astype(jnp.float32)
    scale = 1.0 / jnp.sqrt(jnp.float32(length))
    cosine = jnp.cos(theta) * scale
    sine = jnp.sin(theta) * scale
    real_rows = jnp.stack([cosine, sine], axis=1)
    imag_rows = jnp.stack([-sine, cosine], axis=1)
    return jnp.concatenate([real_rows, imag_rows], axis=0)


def filter_frames(padded, filter_taps, count):
    filtered = jnp.zeros((2, count, padded.shape[2], padded.shape[3]), jnp.float32)
    for tap in range(filter_taps.shape[0]):
        filtered = filtered + filter_taps[tap][None, None, :, None] * padded[
            :, tap : tap + count
        ].astype(jnp.float32)
    return filtered


def transform(filtered, table):
    spectra = jnp.einsum("kcn,cfna->kfa", table, filtered, precision=lax.Precision.HIGHEST)
    return spectra.reshape(2, table.shape[0] // 2, filtered.shape[1], filtered.shape[3])


def on_device(samples, filter_taps):
    nch = filter_taps.shape[1]
    rim = filter_taps.shape[0] - 1
    width = samples.shape[2]
    frames_here = samples.shape[1] // nch
    local = samples.reshape(2, frames_here, nch, width)
    table = dft_table(CH_DEV * lax.axis_size("tm"), nch)
    ahead = passed_along(local[:, :rim], "tm", -1)
    padded = jnp.concatenate([local, ahead], axis=1)
    spectra = transform(filter_frames(padded, filter_taps, frames_here), table)
    spectra = spectra.astype(jnp.bfloat16)
    turned = lax.all_to_all(spectra, "tm", split_axis=1, concat_axis=2, tiled=True)
    scale = 1.0 / turned.shape[2]
    real_part = turned[0]
    imag_part = turned[1]
    left = jnp.concatenate(
        [
            jnp.concatenate([real_part, imag_part], axis=1),
            jnp.concatenate([imag_part, -real_part], axis=1),
        ],
        axis=2,
    )
    right_block = lax.all_gather(turned, "input", axis=3, tiled=True)
    stacked = jnp.concatenate([right_block[0], right_block[1]], axis=1)
    product = jnp.einsum("cfa,cfb->cab", left, stacked, preferred_element_type=jnp.float32) * scale
    product = product.reshape(product.shape[0], 2, width, right_block.shape[3])
    return jnp.transpose(product, (1, 0, 2, 3)).astype(jnp.bfloat16)


def solution(mesh):
    in_specs = (P(None, "tm", "input"), P())
    out_specs = P(None, "tm", "input", None)
    return jax.shard_map(
        on_device, mesh=mesh, in_specs=in_specs, out_specs=out_specs, check_vma=False
    )
```

profile of v0, /device:TPU:8, one launch (start us, length us, event | category | flops | bytes accessed | tf_op | source)
XLA Modules:
  0.0 424.8 jit_solution(3179844550799687338)
XLA Ops:
  6.5 0.0 copy-start
  6.5 0.0 all-gather.2.cloned.1.call-start
  6.5 4.1 slice.146
  10.6 4.0 copy.51
  14.6 1.3 collective-permute-start
  15.9 1.0 fusion.110
  16.9 1.0 sine_multiply_fusion
  17.9 0.0 copy-done
  18.0 7.5 %constant_dynamic-update-slice_fusion.1 = bf16[2,31,1024,128]{3,2,0,1:T(8,128)(2,1)} fusion(bf16[2,16,1024,128]{3,2,1,0:T(8,128)(2,1)} %bitcast.48), kind=kLoop, calls=%fused_computation.116 | loop fusion | bytes 16777216
  25.5 3.7 collective-permute-done
  29.2 7.1 %constant_dynamic-update-slice_fusion = bf16[2,31,1024,128]{3,2,0,1:T(8,128)(2,1)} fusion(bf16[2,31,1024,128]{3,2,0,1:T(8,128)(2,1)} %constant_dynamic-update-slice_fusion.1, bf16[2,15,1024,128]{3,2,0,1:T(8,128)(2,1)} %collective-permute-done), kind=kLoop, calls=%fused_computation.115 | loop fusion | bytes 15728640 | tf_op jit(solution)/shard_map/concatenate | solution.py:50
  36.4 46.7 %fusion.119 = f32[2,16,1024,128]{3,2,0,1:T(8,128)S(1)} fusion(bf16[2,31,1024,128]{3,2,0,1:T(8,128)(2,1)} %constant_dynamic-update-slice_fusion, f32[1024]{0:T(1024)S(1)} %bitcast.71, f32[1024]{0:T(1024)S(1)} %bitcast.72, f32[1024]{0:T(1024)S(1)} %bitcast.58, f32[1024]{0:T(1024)S(1)} %bitcast.59, f32[1024]{0:T(1024)S(1)} %bitcast.60, ...), kind=kLoop, calls=%fused_computation.1.clone.clone.clone.clone.clone.2 | loop fusion | flops 197132288 | bytes 151060480 | tf_op jit(solution)/shard_map/kcn,cfna->kfa/dot_general | solution.py:38
  83.1 8.9 %fusion.88 = bf16[128,16,128]{2,0,1:T(8,128)(2,1)S(1)} fusion(f32[64,1,1024]{2,0,1:T(8,128)S(1)} %get-tuple-element.26, f32[64,1,1024]{2,0,1:T(8,128)S(1)} %fusion.110, f32[64,1,1024]{2,0,1:T(8,128)S(1)} %get-tuple-element.25, f32[2,16,1024,128]{3,2,0,1:T(8,128)S(1)} %fusion.119), kind=kOutput, calls=%fused_computation.88 | convolution fusion | flops 6443499520 | bytes 18087936 | tf_op jit(solution)/shard_map/kcn,cfna->kfa/dot_general | solution.py:38
  92.0 0.3 copy.33
  92.3 192.0 %all_to_all.18 = bf16[2,64,16,128]{3,2,0,1:T(8,128)(2,1)S(1)} all-to-all(bf16[2,64,16,128]{3,2,0,1:T(8,128)(2,1)S(1)} %copy.33), channel_id=1, replica_groups=mesh['tm'=16,'input'=16] {'tm'}, dimensions={1} | all-to-all | bytes 1048576 | tf_op jit(solution)/shard_map/all_to_all | solution.py:53
  284.3 0.8 copy.41
  285.1 0.0 all-gather.2.cloned.1.call-update
  285.3 0.1 copy.37
  285.5 0.1 copy.38
  285.7 123.6 %all-gather.2.cloned.1.call-done = bf16[2,4,256,2048]{3,2,1,0:T(8,128)(2,1)} async-done(((bf16[2,4,256,128]{3,2,1,0:T(8,128)(2,1)}), bf16[2,4,256,2048]{3,2,1,0:T(8,128)(2,1)}) %all-gather.2.cloned.1.call-update) | async-done | bytes 8388624 | tf_op jit(solution)/shard_map/all_gather | solution.py:64
  409.2 3.8 slice_bitcast_fusion.1
  413.0 2.6 multiply_convert_fusion
  415.7 2.3 copy.56
  (6 shorter events, 0.2 us)
Async XLA Ops:
  6.5 11.4 %copy-start = (f32[16,1024]{1,0:T(8,128)S(1)}, f32[16,1024]{1,0:T(8,128)}, u32[]{:S(2)}) copy-start(f32[16,1024]{1,0:T(8,128)} %param.3) | copy-start | bytes 196612
  6.5 402.7 %all-gather.2.cloned.1.call-start = ((), (), s32[]{:S(2)}) async-start(), calls=%async_computation.1 | async-start | bytes 8912896 | tf_op jit(solution)/shard_map/all_gather | solution.py:64
  14.6 14.6 %collective-permute-start = (bf16[2,15,1024,128]{3,2,0,1:T(8,128)(2,1)}, bf16[2,15,1024,128]{3,2,0,1:T(8,128)(2,1)}, u32[]{:S(2)}, u32[]{:S(2)}) collective-permute-start(bf16[2,15,1024,128]{3,2,0,1:T(8,128)(2,1)} %copy.51), channel_id=1, source_target_pairs={{16,0},{32,16},{48,32},{64,48},{80,64},{96,80},{112,96},{128,112},... | collective-permute-start | bytes 23592968 | tf_op jit(solution)/shard_map/ppermute | solution.py:12
Sparse Core Ops, SparseCore 0:
  285.3 123.9 all-gather.1
where the time goes:
time: 425 us
  blocking collectives  192 us (45%)
  waiting for transfers between devices  127 us (30%)
  other arithmetic  48.8 us (11%)
  local copies, waits for them, and re-layouts  30.4 us (7%)
  between operations  13.5 us (3%)
  matrix products  11.5 us (3%)
    all_to_all x1, blocking collectives, on_device(): lax.all_to_all(spectra, 'tm', split_axis=1, concat_axis=2, tiled=True)  192 us
    all_gather x1, waiting for transfers between devices, on_device(): right_block = lax.all_gather(turned, 'input', axis=3, tiled=True)  124 us
    dot_general x1, other arithmetic, transform(): jnp.einsum('kcn,cfna->kfa', table, filtered, precision=lax.Precision.HIGH...  46.7 us
    unnamed x4, local copies, waits for them, and re-layouts  11.5 us
    dot_general x1, matrix products, transform(): jnp.einsum('kcn,cfna->kfa', table, filtered, precision=lax.Precision.HIGH...  8.89 us
  transfers between devices with their start and end apart: 2, of which 2 were waited for; matrix products, arithmetic and copies ran while one was open for 2% of the time, Pallas kernels for 0%

commit v1 on v0

--- a/solution.py
+++ b/solution.py
@@ -61,7 +61,10 @@
         ],
         axis=2,
     )
-    right_block = lax.all_gather(turned, "input", axis=3, tiled=True)
+    devices = lax.axis_size("input")
+    parts = jnp.stack([turned for _ in range(devices)])
+    parts = lax.all_to_all(parts, "input", split_axis=0, concat_axis=0)
+    right_block = jnp.concatenate(parts, axis=3)
     stacked = jnp.concatenate([right_block[0], right_block[1]], axis=1)
     product = jnp.einsum("cfa,cfb->cab", left, stacked, preferred_element_type=jnp.float32) * scale
     product = product.reshape(product.shape[0], 2, width, right_block.shape[3])

time: 425 us -> 512 us (1.20)
  the two profiles are of different devices: /device:TPU:8 before, /device:TPU:64 now
where the time goes in v1:
time: 512 us
  blocking collectives  192 us (38%)
  waiting for transfers between devices  186 us (36%)
  local copies, waits for them, and re-layouts  62.4 us (12%)
  other arithmetic  49.1 us (10%)
  matrix products  13.7 us (3%)
  starting transfers between devices  8.13 us (2%)
    all_to_all x1, blocking collectives, on_device(): lax.all_to_all(spectra, 'tm', split_axis=1, concat_axis=2, tiled=True)  192 us
    all_to_all x1, waiting for transfers between devices, on_device(): parts = lax.all_to_all(parts, 'input', split_axis=0, concat_axis=0)  182 us
    dot_general x1, other arithmetic, transform(): jnp.einsum('kcn,cfna->kfa', table, filtered, precision=lax.Precision.HIGH...  47.1 us
    slice x3, local copies, waits for them, and re-layouts, on_device(): stacked = jnp.concatenate([right_block[0], right_block[1]], axis=1)  16.7 us
    squeeze x2, local copies, waits for them, and re-layouts, on_device(): stacked = jnp.concatenate([right_block[0], right_block[1]], axis=1)  14.6 us
    unnamed x4, local copies, waits for them, and re-layouts  11.5 us
  transfers between devices with their start and end apart: 2, of which 2 were waited for; matrix products, arithmetic and copies ran while one was open for 2% of the time, Pallas kernels for 0%

profile of v1, /device:TPU:64, one launch (start us, length us, event | category | flops | bytes accessed | tf_op | source)
XLA Modules:
  0.0 511.6 jit_solution(9369154438631796447)
XLA Ops:
  0.0 0.0 copy-start
  0.0 4.1 slice.148
  4.1 4.0 copy.52
  8.1 1.3 collective-permute-start
  9.3 1.0 fusion.110
  10.3 1.0 sine_multiply_fusion
  11.4 0.0 copy-done
  11.4 7.5 %constant_dynamic-update-slice_fusion.1 = bf16[2,31,1024,128]{3,2,0,1:T(8,128)(2,1)} fusion(bf16[2,16,1024,128]{3,2,1,0:T(8,128)(2,1)} %bitcast.49), kind=kLoop, calls=%fused_computation.114 | loop fusion | bytes 16777216
  19.0 3.7 collective-permute-done
  22.7 7.1 %constant_dynamic-update-slice_fusion = bf16[2,31,1024,128]{3,2,0,1:T(8,128)(2,1)} fusion(bf16[2,31,1024,128]{3,2,0,1:T(8,128)(2,1)} %constant_dynamic-update-slice_fusion.1, bf16[2,15,1024,128]{3,2,0,1:T(8,128)(2,1)} %collective-permute-done), kind=kLoop, calls=%fused_computation.113 | loop fusion | bytes 15728640 | tf_op jit(solution)/shard_map/concatenate | solution.py:50
  29.8 47.1 %fusion.120 = f32[2,16,1024,128]{3,2,0,1:T(8,128)S(1)} fusion(bf16[2,31,1024,128]{3,2,0,1:T(8,128)(2,1)} %constant_dynamic-update-slice_fusion, f32[1024]{0:T(1024)S(1)} %bitcast.72, f32[1024]{0:T(1024)S(1)} %bitcast.73, f32[1024]{0:T(1024)S(1)} %bitcast.59, f32[1024]{0:T(1024)S(1)} %bitcast.60, f32[1024]{0:T(1024)S(1)} %bitcast.61, ...), kind=kLoop, calls=%fused_computation.1.clone.clone.clone.clone.clone.2 | loop fusion | flops 197132288 | bytes 151060480 | tf_op jit(solution)/shard_map/kcn,cfna->kfa/dot_general | solution.py:38
  76.9 8.9 %fusion.88 = bf16[128,16,128]{2,0,1:T(8,128)(2,1)S(1)} fusion(f32[64,1,1024]{2,0,1:T(8,128)S(1)} %get-tuple-element.26, f32[64,1,1024]{2,0,1:T(8,128)S(1)} %fusion.110, f32[64,1,1024]{2,0,1:T(8,128)S(1)} %get-tuple-element.25, f32[2,16,1024,128]{3,2,0,1:T(8,128)S(1)} %fusion.120), kind=kOutput, calls=%fused_computation.86 | convolution fusion | flops 6443499520 | bytes 18087936 | tf_op jit(solution)/shard_map/kcn,cfna->kfa/dot_general | solution.py:38
  85.8 0.3 copy.32
  86.1 192.2 %all_to_all.20 = bf16[2,64,16,128]{3,2,0,1:T(8,128)(2,1)S(1)} all-to-all(bf16[2,64,16,128]{3,2,0,1:T(8,128)(2,1)S(1)} %copy.32), channel_id=1, replica_groups=mesh['tm'=16,'input'=16] {'tm'}, dimensions={1} | all-to-all | bytes 1048576 | tf_op jit(solution)/shard_map/all_to_all | solution.py:53
  278.4 5.3 %stack.11 = bf16[16,2,4,256,128]{4,3,2,1,0:T(8,128)(2,1)} broadcast(bf16[2,4,256,128]{3,2,1,0:T(8,128)(2,1)S(1)} %bitcast.54), dimensions={1,2,3,4} | broadcast | bytes 8912896 | tf_op jit(solution)/shard_map/stack | solution.py:65
  283.7 6.8 %all-to-all-start.1 = ((bf16[16,2,4,256,128]{4,3,2,1,0:T(8,128)(2,1)}), bf16[16,2,4,256,128]{4,3,2,1,0:T(8,128)(2,1)}, u32[]{:S(2)}, u32[]{:S(2)}) async-start(bf16[16,2,4,256,128]{4,3,2,1,0:T(8,128)(2,1)} %stack.11), calls=%async_computation.1 | async-start | bytes 16777216 | tf_op jit(solution)/shard_map/all_to_all | solution.py:66
  290.6 0.1 copy.36
  290.9 0.1 copy.37
  291.0 182.2 %all-to-all-done.1 = bf16[16,2,4,256,128]{4,3,2,1,0:T(8,128)(2,1)} async-done(((bf16[16,2,4,256,128]{4,3,2,1,0:T(8,128)(2,1)}), bf16[16,2,4,256,128]{4,3,2,1,0:T(8,128)(2,1)}, u32[]{:S(2)}, u32[]{:S(2)}) %all-to-all-start.1) | async-done | bytes 8388640 | tf_op jit(solution)/shard_map/all_to_all | solution.py:66
  473.2 5.2 %fusion.114 = (bf16[1,4,256,16,128]{4,2,1,0,3:T(8,128)(2,1)S(1)}, bf16[1,4,256,16,128]{4,2,1,0,3:T(8,128)(2,1)}) fusion(bf16[2,4,256,16,128]{4,2,1,0,3:T(8,128)(2,1)} %bitcast.28), kind=kLoop, calls=%fused_computation.118 | loop fusion | bytes 16777216 | tf_op jit(solution)/shard_map/slice | solution.py:68
  478.4 4.7 copy.41
  483.1 7.3 %squeeze.14 = bf16[4,256,2048]{2,1,0:T(8,128)(2,1)} reshape(bf16[1,4,256,16,128]{4,3,2,1,0:T(8,128)(2,1)} %copy.41) | data formatting | bytes 8388608 | tf_op jit(solution)/shard_map/squeeze | solution.py:68
  490.4 6.9 %copy.42 = bf16[1,4,256,16,128]{4,3,2,1,0:T(8,128)(2,1)} copy(bf16[1,4,256,16,128]{4,2,1,0,3:T(8,128)(2,1)} %get-tuple-element.6) | data formatting | bytes 8388608 | tf_op jit(solution)/shard_map/slice | solution.py:68
  497.2 7.3 %squeeze.15 = bf16[4,256,2048]{2,1,0:T(8,128)(2,1)} reshape(bf16[1,4,256,16,128]{4,3,2,1,0:T(8,128)(2,1)} %copy.42) | data formatting | bytes 8388608 | tf_op jit(solution)/shard_map/squeeze | solution.py:68
  504.5 4.8 multiply_convert_fusion
  509.3 2.3 copy.57
  (7 shorter events, 0.2 us)
Async XLA Ops:
  0.0 11.4 %copy-start = (f32[16,1024]{1,0:T(8,128)S(1)}, f32[16,1024]{1,0:T(8,128)}, u32[]{:S(2)}) copy-start(f32[16,1024]{1,0:T(8,128)} %param.3) | copy-start | bytes 196612
  8.1 14.6 %collective-permute-start = (bf16[2,15,1024,128]{3,2,0,1:T(8,128)(2,1)}, bf16[2,15,1024,128]{3,2,0,1:T(8,128)(2,1)}, u32[]{:S(2)}, u32[]{:S(2)}) collective-permute-start(bf16[2,15,1024,128]{3,2,0,1:T(8,128)(2,1)} %copy.52), channel_id=1, source_target_pairs={{16,0},{32,16},{48,32},{64,48},{80,64},{96,80},{112,96},{128,112},... | collective-permute-start | bytes 23592968 | tf_op jit(solution)/shard_map/ppermute | solution.py:12
  283.7 189.6 %all-to-all-start.1 = ((bf16[16,2,4,256,128]{4,3,2,1,0:T(8,128)(2,1)}), bf16[16,2,4,256,128]{4,3,2,1,0:T(8,128)(2,1)}, u32[]{:S(2)}, u32[]{:S(2)}) async-start(bf16[16,2,4,256,128]{4,3,2,1,0:T(8,128)(2,1)} %stack.11), calls=%async_computation.1 | async-start | bytes 16777216 | tf_op jit(solution)/shard_map/all_to_all | solution.py:66
